TPU v7x, 512 devices: a whole 4x8x8 slice. The times are simulated.
512 devices in a mesh: grow: 64 (over y, z_lo, core), trans: 8 (over z_hi, x).
Axes of the slice: x: 4, y: 8, z: 8 (z_hi: 2, z_lo: 4; z = z_hi * 4 + z_lo), core: 2. Of those that a mesh axis runs over, the one named last changes fastest.
Arguments:
- phase_label: int32 [1536, 64, 128], P('grow', 'trans'), may hold values from 0 to 3
- grain_label: int32 [1536, 64, 128], P('grow', 'trans'), may hold values from 0 to 31
- grain_orient: int32 [32], replicated, may hold values from 0 to 7
- orient_mobility: float32 [8], replicated, may hold values from 0.4 to 1.2
- solute_init: float32 [2, 1536, 64, 128], P(None, 'grow', 'trans'), may hold values from 0.1 to 0.5
- partition: float32 [4, 2], replicated, may hold values from -0.5 to 0.5
Outputs:
- phase_out: float32 [4, 1536, 64, 128], P(None, 'grow', 'trans')
- solute_out: float32 [2, 1536, 64, 128], P(None, 'grow', 'trans')
All inputs are finite; a program needn't handle non-finite values.
Results may differ from a plain program's by a relative error of at most 0.00002.
Values sent between devices are 32-bit elements; how exact they have to be, the bound alone decides.
A program may use at most 64 MiB of HBM per device.

v0:
```python
import jax
import jax.numpy as jnp
from jax import lax
from jax.sharding import PartitionSpec as P

SHIFT = 16


ANISOTROPY = 1.5
WELL_HEIGHT = 4.0
TIME_STEP = 0.06
LIQUID_DIFFUSION = 1.0
SOLID_DIFFUSION = 0.1
COOLING_WEIGHTS = (-1.0, 0.8, 0.7, 0.6)
FIRST_WEIGHTS = (0.5, -1.0, 0.4, 0.3)
SECOND_WEIGHTS = (0.4, 0.3, -1.0, 0.5)
INFLOW_FIRST = 0.3
INFLOW_SECOND = 0.2
LIQUID_MOBILITY = 1.0


def padded_2(cells, sides, width):
    for axis, dim in sides:
        count = lax.axis_size(axis)
        head = lax.slice_in_dim(cells, 0, width, axis=dim)
        tail = lax.slice_in_dim(cells, cells.shape[dim] - width, cells.shape[dim], axis=dim)
        cells = jnp.concatenate(
            [
                lax.ppermute(tail, axis, [(i, (i + 1) % count) for i in range(count)]),
                cells,
                lax.ppermute(head, axis, [((i + 1) % count, i) for i in range(count)]),
            ],
            axis=dim,
        )
    return cells


def from_behind(value, axis, steps):
    count = lax.axis_size(axis)
    initial, last = (max(0, -steps), min(count, count - steps))
    return lax.ppermute(value, axis, [(source, source + steps) for source in range(initial, last)])


def advance(padded, mobility, undercool, partition):
    centre = padded[:, 1:-1, 1:-1]
    plane_up = padded[:, 2:, 1:-1]
    plane_down = padded[:, :-2, 1:-1]
    row_next = padded[:, 1:-1, 2:]
    row_prev = padded[:, 1:-1, :-2]
    col_next = jnp.roll(centre, -1, axis=3)
    col_prev = jnp.roll(centre, 1, axis=3)
    phases = centre[:4]
    solutes = centre[4:]
    laplace = ANISOTROPY * (plane_up[:4] + plane_down[:4] - 2.0 * phases)
    laplace = laplace + (row_next[:4] + row_prev[:4] - 2.0 * phases)
    laplace = laplace + (col_next[:4] + col_prev[:4] - 2.0 * phases)
    cooling_w = jnp.array(COOLING_WEIGHTS, dtype=phases.dtype).reshape(4, 1, 1, 1)
    first_w = jnp.array(FIRST_WEIGHTS, dtype=phases.dtype).reshape(4, 1, 1, 1)
    second_w = jnp.array(SECOND_WEIGHTS, dtype=phases.dtype).reshape(4, 1, 1, 1)
    driving = cooling_w * undercool[None] + first_w * solutes[0][None] + second_w * solutes[1][None]
    forcing = laplace + WELL_HEIGHT * phases * (1.0 - phases) * (phases - 0.5 + driving)
    growth_rate = mobility[None] * (forcing - jnp.mean(forcing, axis=0, keepdims=True))
    trials = jnp.clip(phases + TIME_STEP * growth_rate, 0.0, 1.0)
    new_phases = trials / jnp.sum(trials, axis=0, keepdims=True)
    own_diffusion = SOLID_DIFFUSION + (LIQUID_DIFFUSION - SOLID_DIFFUSION) * centre[0]
    influx = jnp.zeros_like(solutes)
    for neighbour in (plane_up, plane_down, row_next, row_prev, col_next, col_prev):
        other = SOLID_DIFFUSION + (LIQUID_DIFFUSION - SOLID_DIFFUSION) * neighbour[0]
        influx = influx + 0.5 * (other + own_diffusion)[None] * (neighbour[4:] - solutes)
    changes = new_phases - phases
    rejected = partition[0][:, None, None, None] * changes[0][None]
    rejected = rejected + partition[1][:, None, None, None] * changes[1][None]
    rejected = rejected + partition[2][:, None, None, None] * changes[2][None]
    rejected = rejected + partition[3][:, None, None, None] * changes[3][None]
    new_solutes = solutes + TIME_STEP * influx - rejected
    return jnp.concatenate([new_phases, new_solutes], axis=0)


def fix_ends(padded, margin, first_slab, last_slab):
    lower_edge = padded[:, margin : margin + 1]
    upper_edge = padded[:, -margin - 1 : -margin]
    lower_ghost = jnp.where(first_slab, lower_edge, padded[:, :margin])
    upper_ghost = jnp.where(last_slab, upper_edge, padded[:, -margin:])
    return jnp.concatenate([lower_ghost, padded[:, margin:-margin], upper_ghost], axis=1)


def cooling(heights, total_depth):
    return (2.0 * (0.5 - (heights + 0.5) / total_depth))[:, None, None]


def side_rims(fields):
    return padded_2(fields, (("trans", 2),), 1)


def window_step(window, base, total_depth, last_slab, partition):
    length = window.shape[1]
    offsets = jnp.arange(length, dtype=jnp.int32)
    top_offset = jnp.clip(total_depth - 1 - base, 0, length - 1)
    edge = lax.dynamic_slice_in_dim(window, top_offset, 1, 1)
    beyond = jnp.logical_and(last_slab, offsets > top_offset)[None, :, None, None]
    window = jnp.where(beyond, edge, window)
    padded = side_rims(window[:6])
    heights = (base + 1 + jnp.arange(length - 2, dtype=jnp.int32)).astype(window.dtype)
    stepped = advance(padded, window[6, 1:-1], cooling(heights, total_depth), partition)
    return jnp.concatenate([stepped, window[6:, 1:-1]], axis=0)


def final_step(window, undercool, partition):
    padded = side_rims(window[:6])
    return advance(padded, window[6, 1:-1], undercool, partition)


def shards(phase_label, grain_label, grain_orient, orient_mobility, solute_init, partition):
    slab_index = lax.axis_index("grow")
    slab_count = lax.axis_size("grow")
    planes = phase_label.shape[0]
    first_slab = slab_index == 0
    last_slab = slab_index == slab_count - 1
    orients = orient_mobility.shape[0]
    grains = grain_orient.shape[0]
    orient_ids = jnp.arange(orients, dtype=jnp.int32)
    grain_mobility = jnp.sum(
        jnp.where(grain_orient[:, None] == orient_ids[None, :], orient_mobility[None, :], 0.0),
        axis=1,
    )
    grain_ids = jnp.arange(grains, dtype=jnp.int32)[:, None, None, None]
    mobility = jnp.sum(
        jnp.where(grain_label[None] == grain_ids, grain_mobility[:, None, None, None], 0.0), axis=0
    )
    labels = jnp.arange(4, dtype=jnp.int32)[:, None, None, None]
    phases = (phase_label[None] == labels).astype(solute_init.dtype)
    fields = jnp.concatenate([phases, solute_init], axis=0)
    total_depth = planes * slab_count
    heights = (slab_index * planes + jnp.arange(planes, dtype=jnp.int32)).astype(fields.dtype)
    undercool = cooling(heights, total_depth)
    inflow = jnp.array(
        [1.0, 0.0, 0.0, 0.0, INFLOW_FIRST, INFLOW_SECOND, LIQUID_MOBILITY], dtype=fields.dtype
    )
    stacked = jnp.concatenate([fields, mobility[None]], axis=0)
    received = from_behind(stacked[:, : SHIFT + 3], "grow", -1)
    window = jnp.concatenate([stacked[:, SHIFT - 3 :], received], axis=1)
    base = slab_index * planes + SHIFT - 3
    for turn in range(2):
        window = window_step(window, base + turn, total_depth, last_slab, partition)
    new_index = slab_index * planes - 1 + jnp.arange(window.shape[1], dtype=jnp.int32)
    liquid_mask = (new_index >= total_depth - SHIFT)[None, :, None, None]
    window = jnp.where(liquid_mask, inflow[:, None, None, None], window)
    window = fix_ends(window, 1, first_slab, last_slab)
    fields = final_step(window, undercool, partition)
    return (fields[:4], fields[4:])


def solution(mesh):
    placed = (
        P("grow", "trans", None),
        P("grow", "trans", None),
        P(),
        P(),
        P(None, "grow", "trans", None),
        P(),
    )
    return jax.shard_map(
        shards,
        mesh=mesh,
        in_specs=placed,
        out_specs=(P(None, "grow", "trans", None), P(None, "grow", "trans", None)),
        check_vma=False,
    )
```

profile of v0, /device:TPU:97, one launch (start us, length us, event | category | flops | bytes accessed | tf_op | source)
XLA Modules:
  0.0 80.5 jit_solution(801224584161822712)
XLA Ops:
  0.6 0.9 %fusion.34 = f32[4,24,8,128]{3,2,1,0:T(8,128)S(1)} fusion(s32[24,8,128]{2,1,0:T(8,128)} %param.16), kind=kLoop, calls=%fused_computation.87 | loop fusion | flops 196608 | bytes 491520 | tf_op jit(solution)/shard_map/convert_element_type | solution.py:131
  1.6 0.0 copy-start.4
  1.6 0.8 select_reduce_fusion.1
  2.4 1.3 %select_reduce_fusion = f32[24,8,128]{2,1,0:T(8,128)S(1)} fusion(f32[32]{0:T(128)S(1)} %select_reduce_fusion.1, s32[24,8,128]{2,1,0:T(8,128)} %param.17), kind=kLoop, calls=%fused_computation | loop fusion | flops 2334720 | bytes 196736 | tf_op jit(solution)/shard_map/reduce_sum | solution.py:127
  3.7 1.0 %pad_maximum_fusion.4 = f32[7,19,8,128]{3,2,1,0:T(8,128)S(1)} fusion(f32[1,24,8,128]{3,2,1,0:T(8,128)S(1)} %bitcast.83, f32[2,24,8,128]{3,2,1,0:T(8,128)} %param.20, f32[4,24,8,128]{3,2,1,0:T(8,128)S(1)} %fusion.34), kind=kLoop, calls=%fused_computation.40 | loop fusion | flops 272384 | bytes 1232896 | tf_op jit(solution)/shard_map/concatenate | solution.py:139
  4.6 2.6 %collective-permute-start = (f32[7,19,8,128]{3,2,1,0:T(8,128)S(1)}, f32[7,19,8,128]{3,2,1,0:T(8,128)S(1)}, u32[]{:S(2)}, u32[]{:S(2)}) collective-permute-start(f32[7,19,8,128]{3,2,1,0:T(8,128)S(1)} %pad_maximum_fusion.4), channel_id=1, source_target_pairs={{8,0},{16,8},{24,16},{32,24},{40,32},{48,40},{56,48},{64,56},{72,6... | collective-permute-start | bytes 1634312 | tf_op jit(solution)/shard_map/ppermute | solution.py:41
  7.3 0.2 slice_reduce_fusion.3
  7.6 0.1 broadcast_multiply_fusion.5
  7.6 0.1 broadcast_multiply_fusion.4
  7.7 0.1 broadcast_multiply_fusion.3
  7.8 8.5 %collective-permute-done = f32[7,19,8,128]{3,2,1,0:T(8,128)S(1)} collective-permute-done((f32[7,19,8,128]{3,2,1,0:T(8,128)S(1)}, f32[7,19,8,128]{3,2,1,0:T(8,128)S(1)}, u32[]{:S(2)}, u32[]{:S(2)}) %collective-permute-start) | collective-permute-done | bytes 544800 | tf_op jit(solution)/shard_map/ppermute | solution.py:41
  16.3 0.1 fusion
  16.3 0.1 broadcast_select_fusion
  16.5 0.2 fusion.192
  16.7 0.1 fusion.191
  16.9 11.0 %collective-permute-start.1 = (f32[6,30,1,128]{3,1,2,0:T(8,128)S(1)}, f32[6,30,1,128]{3,1,2,0:T(8,128)S(1)}, u32[]{:S(2)}, u32[]{:S(2)}) collective-permute-start(f32[6,30,1,128]{3,1,2,0:T(8,128)S(1)} %copy.34), channel_id=1, source_target_pairs={{1,0},{2,1},{3,2},{4,3},{5,4},{6,5},{7,6},{0,7},{9,8},{10,9},{11,1... | collective-permute-start | bytes 276488 | tf_op jit(solution)/shard_map/ppermute | solution.py:31
  27.9 1.9 %collective-permute-start.2 = (f32[6,30,1,128]{3,1,2,0:T(8,128)S(1)}, f32[6,30,1,128]{3,1,2,0:T(8,128)S(1)}, u32[]{:S(2)}, u32[]{:S(2)}) collective-permute-start(f32[6,30,1,128]{3,1,2,0:T(8,128)S(1)} %copy.36), channel_id=1, source_target_pairs={{0,1},{1,2},{2,3},{3,4},{4,5},{5,6},{6,7},{7,0},{8,9},{9,10},{10,1... | collective-permute-start | bytes 276488 | tf_op jit(solution)/shard_map/ppermute | solution.py:29
  29.9 0.2 fusion.193
  30.2 0.1 copy.35
  30.3 10.6 %collective-permute-done.2 = f32[6,30,1,128]{3,1,2,0:T(8,128)S(1)} collective-permute-done((f32[6,30,1,128]{3,1,2,0:T(8,128)S(1)}, f32[6,30,1,128]{3,1,2,0:T(8,128)S(1)}, u32[]{:S(2)}, u32[]{:S(2)}) %collective-permute-start.2) | collective-permute-done | bytes 92192 | tf_op jit(solution)/shard_map/ppermute | solution.py:29
  40.9 0.1 copy.37
  41.0 0.0 copy-start.2
  41.0 0.0 copy-start.3
  41.0 0.2 fusion.119
  41.2 0.5 copy-done.2
  41.7 0.0 copy-done.3
  41.7 0.7 fusion.189
  42.4 0.1 fusion.184
  42.5 0.1 slice_subtract_fusion
  42.7 0.4 fusion.40
  43.1 0.1 pad_maximum_fusion.2
  43.1 0.1 broadcast_select_fusion.1
  43.3 0.2 fusion.195
  43.5 0.1 fusion.194
  43.6 1.9 %collective-permute-start.3 = (f32[6,28,1,128]{3,1,2,0:T(8,128)S(1)}, f32[6,28,1,128]{3,1,2,0:T(8,128)S(1)}, u32[]{:S(2)}, u32[]{:S(2)}) collective-permute-start(f32[6,28,1,128]{3,1,2,0:T(8,128)S(1)} %copy.38), channel_id=1, source_target_pairs={{1,0},{2,1},{3,2},{4,3},{5,4},{6,5},{7,6},{0,7},{9,8},{10,9},{11,1... | collective-permute-start | bytes 258056 | tf_op jit(solution)/shard_map/ppermute | solution.py:31
  45.6 3.4 %collective-permute-start.4 = (f32[6,28,1,128]{3,1,2,0:T(8,128)S(1)}, f32[6,28,1,128]{3,1,2,0:T(8,128)S(1)}, u32[]{:S(2)}, u32[]{:S(2)}) collective-permute-start(f32[6,28,1,128]{3,1,2,0:T(8,128)S(1)} %copy.40), channel_id=1, source_target_pairs={{0,1},{1,2},{2,3},{3,4},{4,5},{5,6},{6,7},{7,0},{8,9},{9,10},{10,1... | collective-permute-start | bytes 258056 | tf_op jit(solution)/shard_map/ppermute | solution.py:29
  48.9 0.2 fusion.196
  49.2 0.5 collective-permute-done.3
  49.7 0.1 copy.39
  49.8 8.9 %collective-permute-done.4 = f32[6,28,1,128]{3,1,2,0:T(8,128)S(1)} collective-permute-done((f32[6,28,1,128]{3,1,2,0:T(8,128)S(1)}, f32[6,28,1,128]{3,1,2,0:T(8,128)S(1)}, u32[]{:S(2)}, u32[]{:S(2)}) %collective-permute-start.4) | collective-permute-done | bytes 86048 | tf_op jit(solution)/shard_map/ppermute | solution.py:29
  58.8 0.1 copy.41
  58.8 0.2 fusion.148
  59.0 0.6 fusion.187
  59.7 0.1 fusion.183
  59.8 0.1 slice_subtract_fusion.1
  59.9 0.0 copy-start.5
  59.9 0.3 fusion.58
  60.3 0.3 copy-done.5
  60.6 0.1 maximum_select_fusion
  60.8 0.2 fusion.197
  61.0 0.2 fusion.198
  61.3 0.1 pad_maximum_fusion.21
  61.4 1.9 %collective-permute-start.5 = (f32[6,26,1,128]{3,1,2,0:T(8,128)S(1)}, f32[6,26,1,128]{3,1,2,0:T(8,128)S(1)}, u32[]{:S(2)}, u32[]{:S(2)}) collective-permute-start(f32[6,26,1,128]{3,1,2,0:T(8,128)S(1)} %copy.42), channel_id=1, source_target_pairs={{1,0},{2,1},{3,2},{4,3},{5,4},{6,5},{7,6},{0,7},{9,8},{10,9},{11,1... | collective-permute-start | bytes 239624 | tf_op jit(solution)/shard_map/ppermute | solution.py:31
  63.3 3.4 %collective-permute-start.6 = (f32[6,26,1,128]{3,1,2,0:T(8,128)S(1)}, f32[6,26,1,128]{3,1,2,0:T(8,128)S(1)}, u32[]{:S(2)}, u32[]{:S(2)}) collective-permute-start(f32[6,26,1,128]{3,1,2,0:T(8,128)S(1)} %copy.44), channel_id=1, source_target_pairs={{0,1},{1,2},{2,3},{3,4},{4,5},{5,6},{6,7},{7,0},{8,9},{9,10},{10,1... | collective-permute-start | bytes 239624 | tf_op jit(solution)/shard_map/ppermute | solution.py:29
  66.7 0.1 pad_maximum_fusion.3
  66.8 1.0 %collective-permute-done.5 = f32[6,26,1,128]{3,1,2,0:T(8,128)S(1)} collective-permute-done((f32[6,26,1,128]{3,1,2,0:T(8,128)S(1)}, f32[6,26,1,128]{3,1,2,0:T(8,128)S(1)}, u32[]{:S(2)}, u32[]{:S(2)}) %collective-permute-start.5) | collective-permute-done | bytes 79904 | tf_op jit(solution)/shard_map/ppermute | solution.py:31
  67.8 0.1 copy.43
  67.9 9.8 %collective-permute-done.6 = f32[6,26,1,128]{3,1,2,0:T(8,128)S(1)} collective-permute-done((f32[6,26,1,128]{3,1,2,0:T(8,128)S(1)}, f32[6,26,1,128]{3,1,2,0:T(8,128)S(1)}, u32[]{:S(2)}, u32[]{:S(2)}) %collective-permute-start.6) | collective-permute-done | bytes 79904 | tf_op jit(solution)/shard_map/ppermute | solution.py:29
  77.7 0.1 copy.45
  77.7 0.2 fusion.172
  77.9 0.6 fusion.185
  78.5 0.1 fusion.182
  78.6 0.9 %slice_subtract_fusion.2 = (f32[4,24,8,128]{3,2,1,0:T(8,128)S(1)}, f32[4,24,8,128]{3,2,1,0:T(8,128)}) fusion(f32[7,26,8,128]{3,2,1,0:T(8,128)S(1)} %maximum_select_fusion, f32[24,8,128]{2,1,0:T(8,128)S(1)} %fusion.182, f32[4,24,8,128]{3,2,1,0:T(8,128)S(1)} %get-tuple-element.11, f32[24,8,128]{2,1,0:T(8,128)S(1)} %broadcast_multiply_fusion.2, ...), kind=kLoop, calls=%fused_computation.89 | loop fusion | flops 688128 | bytes 1867776 | tf_op jit(solution)/shard_map/sub | solution.py:70
  79.5 1.0 %fusion.76 = f32[2,24,8,128]{3,2,1,0:T(8,128)} fusion(f32[6,24,8,127]{3,2,1,0:T(8,128)S(1)} %get-tuple-element.70, f32[6,24,8,1]{3,2,1,0:T(8,128)S(1)} %get-tuple-element.72, f32[6,24,8,1]{3,2,1,0:T(8,128)S(1)} %get-tuple-element.71, f32[6,24,8,127]{3,2,1,0:T(8,128)S(1)} %get-tuple-element.69, f32[6,26,8,128]{3,2,1,0:T(8,128)S(1)} %slice.668, ...), kind=kLoop, calls=%fused_computation.146 | loop fusion | flops 1622016 | bytes 4100128 | tf_op jit(solution)/shard_map/sub | solution.py:75
  (34 shorter events, 0.5 us)
Async XLA Ops:
  0.6 6.6 %copy-start.1 = (f32[4,2]{0,1:T(2,128)S(1)}, f32[4,2]{0,1:T(2,128)}, u32[]{:S(2)}) copy-start(f32[4,2]{0,1:T(2,128)} %param.21) | copy-start | bytes 100
  1.6 6.0 %copy-start.4 = (f32[4]{0:T(128)S(1)}, f32[4]{0:T(128)}, u32[]{:S(2)}) copy-start(f32[4]{0:T(128)} %constant.55.clone) | copy-start | bytes 52
  1.6 14.7 %copy-start = (f32[2,24,8,128]{3,2,1,0:T(8,128)S(1)}, f32[2,24,8,128]{3,2,1,0:T(8,128)}, u32[]{:S(2)}) copy-start(f32[2,24,8,128]{3,2,1,0:T(8,128)} %param.20) | copy-start | bytes 589828
  4.6 11.6 %collective-permute-start = (f32[7,19,8,128]{3,2,1,0:T(8,128)S(1)}, f32[7,19,8,128]{3,2,1,0:T(8,128)S(1)}, u32[]{:S(2)}, u32[]{:S(2)}) collective-permute-start(f32[7,19,8,128]{3,2,1,0:T(8,128)S(1)} %pad_maximum_fusion.4), channel_id=1, source_target_pairs={{8,0},{16,8},{24,16},{32,24},{40,32},{48,40},{56,48},{64,56},{72,6... | collective-permute-start | bytes 1634312 | tf_op jit(solution)/shard_map/ppermute | solution.py:41
  16.9 13.3 %collective-permute-start.1 = (f32[6,30,1,128]{3,1,2,0:T(8,128)S(1)}, f32[6,30,1,128]{3,1,2,0:T(8,128)S(1)}, u32[]{:S(2)}, u32[]{:S(2)}) collective-permute-start(f32[6,30,1,128]{3,1,2,0:T(8,128)S(1)} %copy.34), channel_id=1, source_target_pairs={{1,0},{2,1},{3,2},{4,3},{5,4},{6,5},{7,6},{0,7},{9,8},{10,9},{11,1... | collective-permute-start | bytes 276488 | tf_op jit(solution)/shard_map/ppermute | solution.py:31
  27.9 13.0 %collective-permute-start.2 = (f32[6,30,1,128]{3,1,2,0:T(8,128)S(1)}, f32[6,30,1,128]{3,1,2,0:T(8,128)S(1)}, u32[]{:S(2)}, u32[]{:S(2)}) collective-permute-start(f32[6,30,1,128]{3,1,2,0:T(8,128)S(1)} %copy.36), channel_id=1, source_target_pairs={{0,1},{1,2},{2,3},{3,4},{4,5},{5,6},{6,7},{7,0},{8,9},{9,10},{10,1... | collective-permute-start | bytes 276488 | tf_op jit(solution)/shard_map/ppermute | solution.py:29
  41.0 0.7 copy-start.2
  41.0 0.7 copy-start.3
  43.6 6.1 %collective-permute-start.3 = (f32[6,28,1,128]{3,1,2,0:T(8,128)S(1)}, f32[6,28,1,128]{3,1,2,0:T(8,128)S(1)}, u32[]{:S(2)}, u32[]{:S(2)}) collective-permute-start(f32[6,28,1,128]{3,1,2,0:T(8,128)S(1)} %copy.38), channel_id=1, source_target_pairs={{1,0},{2,1},{3,2},{4,3},{5,4},{6,5},{7,6},{0,7},{9,8},{10,9},{11,1... | collective-permute-start | bytes 258056 | tf_op jit(solution)/shard_map/ppermute | solution.py:31
  45.6 13.2 %collective-permute-start.4 = (f32[6,28,1,128]{3,1,2,0:T(8,128)S(1)}, f32[6,28,1,128]{3,1,2,0:T(8,128)S(1)}, u32[]{:S(2)}, u32[]{:S(2)}) collective-permute-start(f32[6,28,1,128]{3,1,2,0:T(8,128)S(1)} %copy.40), channel_id=1, source_target_pairs={{0,1},{1,2},{2,3},{3,4},{4,5},{5,6},{6,7},{7,0},{8,9},{9,10},{10,1... | collective-permute-start | bytes 258056 | tf_op jit(solution)/shard_map/ppermute | solution.py:29
  59.9 0.7 copy-start.5
  61.4 6.4 %collective-permute-start.5 = (f32[6,26,1,128]{3,1,2,0:T(8,128)S(1)}, f32[6,26,1,128]{3,1,2,0:T(8,128)S(1)}, u32[]{:S(2)}, u32[]{:S(2)}) collective-permute-start(f32[6,26,1,128]{3,1,2,0:T(8,128)S(1)} %copy.42), channel_id=1, source_target_pairs={{1,0},{2,1},{3,2},{4,3},{5,4},{6,5},{7,6},{0,7},{9,8},{10,9},{11,1... | collective-permute-start | bytes 239624 | tf_op jit(solution)/shard_map/ppermute | solution.py:31
  63.3 14.3 %collective-permute-start.6 = (f32[6,26,1,128]{3,1,2,0:T(8,128)S(1)}, f32[6,26,1,128]{3,1,2,0:T(8,128)S(1)}, u32[]{:S(2)}, u32[]{:S(2)}) collective-permute-start(f32[6,26,1,128]{3,1,2,0:T(8,128)S(1)} %copy.44), channel_id=1, source_target_pairs={{0,1},{1,2},{2,3},{3,4},{4,5},{5,6},{6,7},{7,0},{8,9},{9,10},{10,1... | collective-permute-start | bytes 239624 | tf_op jit(solution)/shard_map/ppermute | solution.py:29
where the time goes:
time: 81.1 us; the launch traced here: 80.5 us
  waiting for transfers between devices  39.3 us (48%)
  starting transfers between devices  26.1 us (32%)
  other arithmetic  10.4 us (13%)
  local copies, waits for them, and re-layouts  3.54 us (4%)
  between operations  1.14 us (1%)
    ppermute x3, waiting for transfers between devices, padded_2(): lax.ppermute(tail, axis, [(i, (i + 1) % count) for i in range(count)])  29.3 us
    ppermute x3, starting transfers between devices, padded_2(): lax.ppermute(head, axis, [((i + 1) % count, i) for i in range(count)])  14.9 us
    ppermute x3, starting transfers between devices, padded_2(): lax.ppermute(tail, axis, [(i, (i + 1) % count) for i in range(count)])  8.64 us
    ppermute x1, waiting for transfers between devices, from_behind(): lax.ppermute(value, axis, [(source, source + steps) for source in range(i...  8.49 us
    ppermute x1, starting transfers between devices, from_behind(): lax.ppermute(value, axis, [(source, source + steps) for source in range(i...  2.58 us
    reduce_sum x3, other arithmetic, advance(): jnp.mean(forcing, axis=0, keepdims=True)  1.87 us
    sub x3, other arithmetic, advance(): new_solutes = solutes + TIME_STEP * influx - rejected  1.73 us
  transfers between devices with their start and end apart: 7, of which 6 were waited for; matrix products, arithmetic and copies ran while one was open for 2% of the time, Pallas kernels for 0%

commit v1 on v0

v1 whole, which is shorter than its diff:
```python
import functools

import jax
import jax.numpy as jnp
from jax import lax
from jax.experimental import pallas as pl
from jax.experimental.pallas import tpu as pltpu
from jax.sharding import PartitionSpec as P

MESH = pl.DeviceIdType.MESH
SHIFT = 16
STEPS = 3
ANISOTROPY = 1.5
WELL_HEIGHT = 4.0
TIME_STEP = 0.06
LIQUID_DIFFUSION = 1.0
SOLID_DIFFUSION = 0.1
COOLING_WEIGHTS = (-1.0, 0.8, 0.7, 0.6)
FIRST_WEIGHTS = (0.5, -1.0, 0.4, 0.3)
SECOND_WEIGHTS = (0.4, 0.3, -1.0, 0.5)
INFLOW = (1.0, 0.0, 0.0, 0.0, 0.3, 0.2)
LIQUID_MOBILITY = 1.0
ROWS = 16


def kernel(n_grow, n_trans, parts, ph, gr, so, go, om, pa, pout, sout, PH, GR, CC, S0, MO, T1, T2, loc, send, recv):
    g = lax.axis_index("grow")
    t = lax.axis_index("trans")
    planes, rows, cols = ph.shape
    left = lax.rem(t + n_trans - 1, n_trans)
    right = lax.rem(t + 1, n_trans)
    first, last = g == 0, g == n_grow - 1
    own = planes - SHIFT + STEPS
    skip = planes - own
    more = SHIFT + STEPS
    length = own + more

    barrier = pltpu.get_barrier_semaphore()

    def greet(dg, tt):
        pl.semaphore_signal(barrier, inc=1, device_id={"grow": g + dg, "trans": tt}, device_id_type=MESH)

    greet(0, left)
    greet(0, right)

    @pl.when(jnp.logical_not(last))
    def _():
        greet(1, t)
        greet(1, left)
        greet(1, right)

    local = []
    for n, (src, dst) in enumerate(
        [
            (ph.at[pl.ds(skip, own)], PH.at[pl.ds(0, own), pl.ds(0, rows)]),
            (gr.at[pl.ds(skip, own)], GR.at[pl.ds(0, own), pl.ds(0, rows)]),
            (so.at[:, pl.ds(skip, own)], CC.at[:, pl.ds(0, own), pl.ds(0, rows)]),
        ]
    ):
        copy = pltpu.make_async_copy(src, dst, loc.at[n])
        copy.start()
        local.append(copy)

    count = 0

    def group(src_plane, size, dst_plane, src_row, dst_row, width, dg, tt):
        nonlocal count
        copies = []
        sp, dp = pl.ds(src_plane, size), pl.ds(dst_plane, size)
        sr, dr = pl.ds(src_row, width), pl.ds(dst_row, width)
        for src, dst in (
            (ph.at[sp, sr], PH.at[dp, dr]),
            (gr.at[sp, sr], GR.at[dp, dr]),
            (so.at[:, sp, sr], CC.at[:, dp, dr]),
        ):
            copies.append(
                pltpu.make_async_remote_copy(
                    src_ref=src,
                    dst_ref=dst,
                    send_sem=send.at[count],
                    recv_sem=recv.at[count],
                    device_id={"grow": g + dg, "trans": tt},
                    device_id_type=MESH,
                )
            )
            count += 1
        return copies

    side = group(skip, own, 0, rows - STEPS, ROWS - STEPS, STEPS, 0, right) + group(skip, own, 0, 0, rows, STEPS, 0, left)
    down = group(0, more, own, 0, 0, rows, -1, t)
    down += group(0, more, own, rows - STEPS, ROWS - STEPS, STEPS, -1, right) + group(0, more, own, 0, rows, STEPS, -1, left)

    @pl.when(first)
    def _():
        pl.semaphore_wait(barrier, 2)

    @pl.when(jnp.logical_not(first))
    def _():
        pl.semaphore_wait(barrier, 5)

    for copy in side:
        copy.start()

    @pl.when(jnp.logical_not(first))
    def _():
        for copy in down:
            copy.start()

    lane = lax.broadcasted_iota(jnp.int32, (ROWS, cols), 1)
    table = jnp.zeros((ROWS, cols), jnp.float32)
    for n in range(go.shape[0]):
        table = jnp.where(lane == n, om[go[n]] * TIME_STEP, table)

    for copy in local:
        copy.wait()
    for copy in side:
        copy.wait_recv()

    @pl.when(jnp.logical_not(last))
    def _():
        for copy in down:
            copy.wait_recv()

    def expand(w, _):
        label = PH[w]
        for a in range(4):
            S0[a, w] = jnp.where(label == a, 1.0, 0.0)
        MO[w] = jnp.take_along_axis(table, jnp.bitwise_and(GR[w], go.shape[0] - 1), axis=1)
        return 0

    if "compute" in parts:
        lax.fori_loop(0, length, expand, 0)

    part = [[pa[a, k] for k in range(2)] for a in range(4)]
    spread = (LIQUID_DIFFUSION - SOLID_DIFFUSION) * 0.5 * TIME_STEP
    base = SOLID_DIFFUSION * 0.5 * TIME_STEP

    def advance(load, w, up, down, height, mob, keep):
        total = jnp.float32(n_grow * planes)
        undercool = 2.0 * (0.5 - (height.astype(jnp.float32) + 0.5) / total)

        def roll(v, shift, axis):
            return pltpu.roll(v, shift % v.shape[axis], axis)

        centre = [load(k, w) for k in range(6)]
        above = [load(k, up)[:keep] for k in range(6)]
        below = [load(k, down)[:keep] for k in range(6)]
        rown = [roll(v, -1, 0)[:keep] for v in centre]
        rowp = [roll(v, 1, 0)[:keep] for v in centre]
        centre = [v[:keep] for v in centre]
        coln = [roll(v, -1, 1) for v in centre]
        colp = [roll(v, 1, 1) for v in centre]
        c0, c1 = centre[4], centre[5]
        forcing = []
        for a in range(4):
            p = centre[a]
            lap = ANISOTROPY * (above[a] + below[a]) + ((rown[a] + rowp[a]) + (coln[a] + colp[a])) - (2.0 * ANISOTROPY + 4.0) * p
            drive = (p + (COOLING_WEIGHTS[a] * undercool - 0.5)) + (FIRST_WEIGHTS[a] * c0 + SECOND_WEIGHTS[a] * c1)
            forcing.append(lap + (WELL_HEIGHT * p) * ((1.0 - p) * drive))
        mean = 0.25 * ((forcing[0] + forcing[1]) + (forcing[2] + forcing[3]))
        trials = [jnp.clip(centre[a] + mob * (forcing[a] - mean), 0.0, 1.0) for a in range(4)]
        scale = 1.0 / ((trials[0] + trials[1]) + (trials[2] + trials[3]))
        new = [v * scale for v in trials]
        changes = [new[a] - centre[a] for a in range(4)]
        own_d = base + spread * centre[0]
        sums = [None, None]
        for near in (above, below, rown, rowp, coln, colp):
            d = own_d + (base + spread * near[0])
            for k in range(2):
                flow = d * (near[4 + k] - centre[4 + k])
                sums[k] = flow if sums[k] is None else sums[k] + flow
        for k in range(2):
            rejected = (part[0][k] * changes[0] + part[1][k] * changes[1]) + (part[2][k] * changes[2] + part[3][k] * changes[3])
            new.append(centre[4 + k] + sums[k] - rejected)
        return new

    top = jnp.where(last, own - 1, length - 1)
    origin = g * planes + skip

    def one(w, _):
        new = advance(lambda k, i: S0[k, i] if k < 4 else CC[k - 4, i], w, jnp.minimum(w + 1, top), w - 1, origin + w, MO[w], ROWS)
        for k in range(6):
            T1[k, w] = new[k]
        return 0

    def two(w, _):
        new = advance(lambda k, i: T1[k, i], w, jnp.minimum(w + 1, top), w - 1, origin + w, MO[w], ROWS)
        for k in range(6):
            T2[k, w] = new[k]
        return 0

    bottom = jnp.where(first, STEPS, 0)

    def three(w, _):
        new = advance(lambda k, i: T2[k, i], w, w + 1, jnp.maximum(w - 1, bottom), g * planes + w - STEPS, MO[w][:rows], rows)
        for k in range(4):
            pout[k, w - STEPS] = new[k]
        for k in range(2):
            sout[k, w - STEPS] = new[4 + k]
        return 0

    if "compute" in parts:
        lax.fori_loop(1, length - 1, one, 0)
        lax.fori_loop(2, length - 2, two, 0)

        @pl.when(last)
        def _():
            def fill(w, _):
                for k in range(6):
                    T2[k, w] = jnp.full((ROWS, cols), INFLOW[k], jnp.float32)
                MO[w] = jnp.full((ROWS, cols), LIQUID_MOBILITY * TIME_STEP, jnp.float32)
                return 0

            lax.fori_loop(own, length, fill, 0)

        lax.fori_loop(3, length - 3, three, 0)

    for copy in side:
        copy.wait_send()

    @pl.when(jnp.logical_not(first))
    def _():
        for copy in down:
            copy.wait_send()


def solution(mesh, parts=("compute",)):
    n_grow, n_trans = mesh.shape["grow"], mesh.shape["trans"]

    def shards(phase_label, grain_label, grain_orient, orient_mobility, solute_init, partition):
        planes, rows, cols = phase_label.shape
        length = planes + 2 * STEPS
        window = (length, ROWS, cols)
        hbm = pl.BlockSpec(memory_space=pl.ANY)
        smem = pl.BlockSpec(memory_space=pltpu.SMEM)
        vmem = pl.BlockSpec(memory_space=pltpu.VMEM)
        f32 = jnp.float32
        return pl.pallas_call(
            functools.partial(kernel, n_grow, n_trans, parts),
            out_shape=(
                jax.ShapeDtypeStruct((4, planes, rows, cols), f32),
                jax.ShapeDtypeStruct((2, planes, rows, cols), f32),
            ),
            in_specs=[hbm, hbm, hbm, smem, smem, smem],
            out_specs=(vmem, vmem),
            scratch_shapes=[
                pltpu.VMEM(window, jnp.int32),
                pltpu.VMEM(window, jnp.int32),
                pltpu.VMEM((2, *window), f32),
                pltpu.VMEM((4, *window), f32),
                pltpu.VMEM(window, f32),
                pltpu.VMEM((6, *window), f32),
                pltpu.VMEM((6, *window), f32),
                pltpu.SemaphoreType.DMA((3,)),
                pltpu.SemaphoreType.DMA((15,)),
                pltpu.SemaphoreType.DMA((15,)),
            ],
            compiler_params=pltpu.CompilerParams(collective_id=0, has_side_effects=True),
        )(phase_label, grain_label, solute_init, grain_orient, orient_mobility, partition)

    placed = (P("grow", "trans", None), P("grow", "trans", None), P(), P(), P(None, "grow", "trans", None), P())
    return jax.shard_map(
        shards,
        mesh=mesh,
        in_specs=placed,
        out_specs=(P(None, "grow", "trans", None), P(None, "grow", "trans", None)),
        check_vma=False,
    )
```

time: 81.1 us -> 44.8 us (0.55)
  the two profiles are of different devices: /device:TPU:97 before, /device:TPU:1 now
where the time goes in v1:
time: 44.8 us; the launch traced here: 44.6 us
  Pallas kernels  40.1 us (90%)
  local copies, waits for them, and re-layouts  3.82 us (9%)
  between operations  0.65 us (1%)
    pallas_call x1, Pallas kernels, shards(): pl.pallas_call(functools.partial(kernel, n_grow, n_trans, parts), out_sha...  40.1 us
    unnamed x5, local copies, waits for them, and re-layouts  3.82 us

profile of v1, /device:TPU:1, one launch (start us, length us, event | category | flops | bytes accessed | tf_op | source)
XLA Modules:
  0.0 44.6 jit_solution(10704354599921994723)
XLA Ops:
  0.6 1.3 %copy.8.pa = f32[4,2]{1,0:T(4,128)} copy(f32[4,2]{0,1:T(2,128)} %param.11) | data formatting | bytes 64 | tf_op args[5]
  2.0 40.1 %shard_map.77 = (f32[4,24,8,128]{3,2,1,0:T(8,128)}, f32[2,24,8,128]{3,2,1,0:T(8,128)}) custom-call(s32[24,8,128]{2,1,0:T(8,128)} %ph.1, s32[24,8,128]{2,1,0:T(8,128)} %gr.1, f32[2,24,8,128]{3,2,1,0:T(8,128)} %so.1, s32[32]{0:T(128)} %go.1, f32[8]{0:T(128)} %om.1, f32[4,2]{1,0:T(4,128)} %copy.8.pa), custom_call_target="tpu_custom_call" | custom-call | tf_op jit(solution)/shard_map/pallas_call | solution.py:238
  42.1 0.0 copy-start
  42.1 1.8 %copy.11 = f32[4,24,8,128]{3,2,1,0:T(8,128)} copy(f32[4,24,8,128]{3,2,1,0:T(8,128)} %get-tuple-element.4) | data formatting | bytes 786432
  43.9 0.0 copy-done
  43.9 0.7 %copy.12 = f32[2,24,8,128]{3,2,1,0:T(8,128)} copy(f32[2,24,8,128]{3,2,1,0:T(8,128)S(1)} %copy-done) | data formatting | bytes 393216
Async XLA Ops:
  42.1 1.8 %copy-start = (f32[2,24,8,128]{3,2,1,0:T(8,128)S(1)}, f32[2,24,8,128]{3,2,1,0:T(8,128)}, u32[]{:S(2)}) copy-start(f32[2,24,8,128]{3,2,1,0:T(8,128)} %get-tuple-element.5) | copy-start | bytes 589828

commit v2 on v1

v2 whole, which is shorter than its diff:
```python
import functools

import jax
import jax.numpy as jnp
from jax import lax
from jax.experimental import pallas as pl
from jax.experimental.pallas import tpu as pltpu
from jax.sharding import PartitionSpec as P

MESH = pl.DeviceIdType.MESH
SHIFT = 16
STEPS = 3
ANISOTROPY = 1.5
WELL_HEIGHT = 4.0
TIME_STEP = 0.06
LIQUID_DIFFUSION = 1.0
SOLID_DIFFUSION = 0.1
COOLING_WEIGHTS = (-1.0, 0.8, 0.7, 0.6)
FIRST_WEIGHTS = (0.5, -1.0, 0.4, 0.3)
SECOND_WEIGHTS = (0.4, 0.3, -1.0, 0.5)
INFLOW = (1.0, 0.0, 0.0, 0.0, 0.3, 0.2)
LIQUID_MOBILITY = 1.0
ROWS, OWN, NEXT = 24, 8, 16
UNROLL_WIDE, UNROLL_SLIM = 3, 5
SPLIT = 9


def kernel(n_grow, n_trans, ph, gr, so, go_h, om_h, pa_h, pout, sout, PC, GC, PL, GL, SL, PN, GN, SN, S0, MO, T1, T2, TB, go, om, pa, loc, send, recv, ready):
    g = lax.axis_index("grow")
    t = lax.axis_index("trans")
    planes, rows, cols = ph.shape
    left = lax.rem(t + n_trans - 1, n_trans)
    right = lax.rem(t + 1, n_trans)
    half = n_trans // 2
    place = lax.rem(t, half)
    first, last = g == 0, g == n_grow - 1
    far_right = place == half - 1
    far_left = jnp.logical_not(far_right)
    end = jnp.logical_or(place == 0, far_right)
    early = jnp.logical_and(end, t < half)
    own = planes - SHIFT + STEPS
    skip = planes - own
    more = SHIFT + STEPS
    length = own + more

    barrier = pltpu.get_barrier_semaphore()

    def greet(dg, tt):
        pl.semaphore_signal(barrier, inc=1, device_id={"grow": g + dg, "trans": tt}, device_id_type=MESH)

    greet(0, left)
    greet(0, right)

    @pl.when(jnp.logical_not(last))
    def _():
        greet(1, left)
        greet(1, right)
        greet(1, t)

    local = [
        pltpu.make_async_copy(src, dst, loc.at[n])
        for n, (src, dst) in enumerate(
            [
                (ph.at[pl.ds(skip, own)], PC.at[pl.ds(0, own)]),
                (gr.at[pl.ds(skip, own)], GC.at[pl.ds(0, own)]),
                (so.at[:, pl.ds(skip, own)], S0.at[pl.ds(4, 2), pl.ds(0, own), pl.ds(OWN, rows)]),
                (go_h, go),
                (om_h, om),
                (pa_h, pa),
            ]
        )
    ]
    for copy in local:
        copy.start()

    count = 0

    def group(pairs, dg, tt):
        nonlocal count
        copies = []
        for src, dst in pairs:
            copies.append(
                pltpu.make_async_remote_copy(
                    src_ref=src,
                    dst_ref=dst,
                    send_sem=send.at[count],
                    recv_sem=recv.at[count],
                    device_id={"grow": g + dg, "trans": tt},
                    device_id_type=MESH,
                )
            )
            count += 1
        return copies

    def halo(labels, grains, solutes, wide, slim, tt):
        pieces = []
        for src, size, dst, dg in (
            (skip + 1, own - 1, 1, 0),
            (0, SPLIT, own, -1),
            (SPLIT, more - 1 - SPLIT, own + SPLIT, -1),
        ):
            sp, dp = pl.ds(src, size), pl.ds(dst, size)
            pairs = (
                (ph.at[sp, wide], labels.at[dp, wide]),
                (so.at[:, sp, wide], solutes.at[:, dp, wide]),
                (gr.at[sp, slim], grains.at[dp, slim]),
            )
            pieces.append(group(pairs, dg, tt))
        return pieces

    sp, dp = pl.ds(0, more), pl.ds(own, more)
    main = group(
        (
            (ph.at[sp], PC.at[dp]),
            (so.at[:, sp], S0.at[pl.ds(4, 2), dp, pl.ds(OWN, rows)]),
            (gr.at[sp], GC.at[dp]),
        ),
        -1,
        t,
    )
    to_left = halo(PN, GN, SN, pl.ds(0, STEPS), pl.ds(0, STEPS - 1), left)
    to_right = halo(PL, GL, SL, pl.ds(rows - STEPS, STEPS), pl.ds(rows - STEPS + 1, STEPS - 1), right)

    inner = jnp.logical_not(first)
    outer = jnp.logical_not(last)

    def start_halo(copies):
        for copy in copies[0]:
            copy.start()

        @pl.when(inner)
        def _():
            for copy in copies[1] + copies[2]:
                copy.start()

    def start_far():
        @pl.when(far_left)
        def _():
            start_halo(to_left)

        @pl.when(far_right)
        def _():
            start_halo(to_right)

    def start_near():
        @pl.when(far_left)
        def _():
            start_halo(to_right)

        @pl.when(far_right)
        def _():
            start_halo(to_left)

        @pl.when(inner)
        def _():
            for copy in main:
                copy.start()

    def meet():
        @pl.when(first)
        def _():
            pl.semaphore_wait(barrier, 2)

        @pl.when(inner)
        def _():
            pl.semaphore_wait(barrier, 5)

    @pl.when(jnp.logical_not(early))
    def _():
        meet()

        @pl.when(place == 1)
        def _():
            pl.semaphore_signal(ready, inc=1, device_id={"grow": g, "trans": left}, device_id_type=MESH)

        @pl.when(place == half - 2)
        def _():
            pl.semaphore_signal(ready, inc=1, device_id={"grow": g, "trans": right}, device_id_type=MESH)

        start_far()

    @pl.when(end)
    def _():
        pl.semaphore_wait(ready, 1)

    start_near()

    for copy in local[3:]:
        copy.wait()
    lane = lax.broadcasted_iota(jnp.int32, (rows, cols), 1)
    table = jnp.zeros((rows, cols), jnp.float32)
    for n in range(go.shape[0]):
        table = jnp.where(lane == n, om[go[n]] * TIME_STEP, table)
    TB[...] = table

    def expand(low, high, row, labels, grains, solutes):
        def body(w, _):
            at = pl.ds(row, rows)
            label = labels[w]
            for a in range(4):
                S0[a, w, at] = jnp.where(label == a, 1.0, 0.0)
            if solutes is not None:
                for k in range(2):
                    S0[4 + k, w, at] = solutes[k, w]
            grain = jnp.bitwise_and(grains[w], go.shape[0] - 1)
            mob = jnp.take_along_axis(TB[...], grain, axis=1)
            MO[w, at] = jnp.where(jnp.logical_and(last, w >= own), LIQUID_MOBILITY * TIME_STEP, mob)
            return 0

        lax.fori_loop(low, high, body, 0, unroll=2)

    part = [[pa[k, a] for k in range(2)] for a in range(4)]
    spread = (LIQUID_DIFFUSION - SOLID_DIFFUSION) * 0.5 * TIME_STEP
    base = SOLID_DIFFUSION * 0.5 * TIME_STEP

    def roll(v, shift):
        return pltpu.roll(v, shift % v.shape[1], 1)

    def advance(load, w, up, down, height, mob):
        total = jnp.float32(n_grow * planes)
        undercool = 2.0 * (0.5 - (height.astype(jnp.float32) + 0.5) / total)
        centre = [load(k, w, 0) for k in range(6)]
        above = [load(k, up, 0) for k in range(6)]
        below = [load(k, down, 0) for k in range(6)]
        rown = [load(k, w, 1) for k in range(6)]
        rowp = [load(k, w, -1) for k in range(6)]
        coln = [roll(v, -1) for v in centre]
        colp = [roll(v, 1) for v in centre[:4]]
        c0, c1 = centre[4], centre[5]
        forcing = []
        for a in range(4):
            p = centre[a]
            lap = ANISOTROPY * (above[a] + below[a]) + ((rown[a] + rowp[a]) + (coln[a] + colp[a])) - (2.0 * ANISOTROPY + 4.0) * p
            drive = (p + (COOLING_WEIGHTS[a] * undercool - 0.5)) + (FIRST_WEIGHTS[a] * c0 + SECOND_WEIGHTS[a] * c1)
            forcing.append(lap + (WELL_HEIGHT * p) * ((1.0 - p) * drive))
        mean = 0.25 * ((forcing[0] + forcing[1]) + (forcing[2] + forcing[3]))
        trials = [jnp.clip(centre[a] + mob * (forcing[a] - mean), 0.0, 1.0) for a in range(4)]
        scale = 1.0 / ((trials[0] + trials[1]) + (trials[2] + trials[3]))
        new = [v * scale for v in trials]
        changes = [new[a] - centre[a] for a in range(4)]
        own_d = 2.0 * base + spread * centre[0]
        sums = [None, None]
        d = own_d + spread * coln[0]
        for k in range(2):
            flow = d * (coln[4 + k] - centre[4 + k])
            sums[k] = flow - roll(flow, 1)
        for near in (above, below, rown, rowp):
            d = own_d + spread * near[0]
            for k in range(2):
                sums[k] = sums[k] + d * (near[4 + k] - centre[4 + k])
        for k in range(2):
            rejected = (part[0][k] * changes[0] + part[1][k] * changes[1]) + (part[2][k] * changes[2] + part[3][k] * changes[3])
            new.append((centre[4 + k] + sums[k]) - rejected)
        return new

    top = jnp.where(last, own - 1, length - 1)
    origin = g * planes + skip

    def one(low, high, row, size, unroll):
        def load(k, i, by):
            at = pl.ds(row + by, size)
            return S0[k, i, at]

        def body(w, _):
            new = advance(load, w, jnp.minimum(w + 1, top), w - 1, origin + w, MO[w, pl.ds(row, size)])
            for k in range(6):
                T1[k, w, pl.ds(row, size)] = new[k]
            return 0

        lax.fori_loop(low, high, body, 0, unroll=unroll)

    def two(low, high, row, size, unroll):
        def load(k, i, by):
            return T1[k, i, pl.ds(row + by, size)]

        def body(w, _):
            new = advance(load, w, jnp.minimum(w + 1, top), w - 1, origin + w, MO[w, pl.ds(row, size)])
            for k in range(6):
                T2[k, w, pl.ds(row, size)] = new[k]
            return 0

        lax.fori_loop(low, high, body, 0, unroll=unroll)

    bottom = jnp.where(first, STEPS, 0)

    def three(low, high, unroll):
        def load(k, i, by):
            return T2[k, i, pl.ds(OWN + by, rows)]

        def body(w, _):
            new = advance(load, w, w + 1, jnp.maximum(w - 1, bottom), g * planes + w - STEPS, MO[w, pl.ds(OWN, rows)])
            for k in range(4):
                pout[k, w - STEPS] = new[k]
            for k in range(2):
                sout[k, w - STEPS] = new[4 + k]
            return 0

        lax.fori_loop(low, high, body, 0, unroll=unroll)

    def flood(low, high):
        @pl.when(last)
        def _():
            def body(w, _):
                for k in range(6):
                    T2[k, w] = jnp.full((ROWS, cols), INFLOW[k], jnp.float32)
                return 0

            lax.fori_loop(max(low, own), high, body, 0)

    def arrive(copies):
        for copy in copies:
            copy.wait_recv()

    def take(pieces, before, near):
        low = (1, own, own + SPLIT)[pieces[0]]
        high = (own, own + SPLIT, length - 1)[pieces[-1]]

        def side(copies, row, buffers):
            def wait():
                for n in pieces:
                    arrive(copies[n])

            if pieces[0] == 0:
                wait()
            else:
                pl.when(outer)(wait)
            expand(low, high, row, *buffers)

        @pl.when(jnp.logical_and(before, far_left if near else far_right))
        def _():
            side(to_left, NEXT, (PN, GN, SN))

        @pl.when(jnp.logical_and(before, far_right if near else far_left))
        def _():
            side(to_right, 0, (PL, GL, SL))

    middle = jnp.logical_not(end)
    always = g >= 0
    wide = 2 * rows
    for copy in local[:3]:
        copy.wait()
    expand(0, own, OWN, PC, GC, None)
    take([0], always, True)
    take([0], middle, False)
    one(1, own - 1, OWN - 2, wide, UNROLL_WIDE)
    two(2, own - 2, OWN - 2, wide, UNROLL_WIDE)

    @pl.when(early)
    def _():
        meet()
        start_far()

    @pl.when(outer)
    def _():
        arrive(main)

    expand(own, length, OWN, PC, GC, None)
    take([1, 2], always, True)
    take([1, 2], middle, False)
    one(own - 1, length - 1, OWN - 2, wide, UNROLL_WIDE)
    two(own - 2, length - 2, OWN - 2, wide, UNROLL_WIDE)

    near = jnp.where(far_right, NEXT + 2 - rows, OWN - 2)
    bounds = (1, own, own + SPLIT, length)
    for n in range(3):
        high = bounds[n + 1]
        lows = [max(bounds[n] - s, s) for s in (1, 2, 3)]
        take([n], end, False)

        @pl.when(end)
        def _():
            one(lows[0], high - 1, near, rows, UNROLL_SLIM)
            two(lows[1], high - 2, near, rows, UNROLL_SLIM)

        if high - 2 > own:
            flood(lows[1], high - 2)
        three(lows[2], high - 3, UNROLL_SLIM)

    for copy in to_left[0] + to_right[0]:
        copy.wait_send()

    @pl.when(inner)
    def _():
        for copy in main + to_left[1] + to_left[2] + to_right[1] + to_right[2]:
            copy.wait_send()


def solution(mesh):
    n_grow, n_trans = mesh.shape["grow"], mesh.shape["trans"]

    def shards(phase_label, grain_label, grain_orient, orient_mobility, solute_init, partition):
        planes, rows, cols = phase_label.shape
        length = planes + 2 * STEPS
        window = (length, ROWS, cols)
        block = (length, rows, cols)
        hbm = pl.BlockSpec(memory_space=pl.ANY)
        vmem = pl.BlockSpec(memory_space=pltpu.VMEM)
        f32, i32 = jnp.float32, jnp.int32
        return pl.pallas_call(
            functools.partial(kernel, n_grow, n_trans),
            out_shape=(
                pltpu.VMEM((4, planes, rows, cols), f32),
                pltpu.VMEM((2, planes, rows, cols), f32),
            ),
            in_specs=[hbm] * 6,
            out_specs=(vmem, vmem),
            scratch_shapes=[
                pltpu.VMEM(block, i32),
                pltpu.VMEM(block, i32),
                pltpu.VMEM(block, i32),
                pltpu.VMEM(block, i32),
                pltpu.VMEM((2, *block), f32),
                pltpu.VMEM(block, i32),
                pltpu.VMEM(block, i32),
                pltpu.VMEM((2, *block), f32),
                pltpu.VMEM((6, *window), f32),
                pltpu.VMEM(window, f32),
                pltpu.VMEM((6, *window), f32),
                pltpu.VMEM((6, *window), f32),
                pltpu.VMEM((rows, cols), f32),
                pltpu.SMEM(grain_orient.shape, i32),
                pltpu.SMEM(orient_mobility.shape, f32),
                pltpu.SMEM(partition.shape[::-1], f32),
                pltpu.SemaphoreType.DMA((6,)),
                pltpu.SemaphoreType.DMA((21,)),
                pltpu.SemaphoreType.DMA((21,)),
                pltpu.SemaphoreType.REGULAR,
            ],
            compiler_params=pltpu.CompilerParams(collective_id=0, has_side_effects=True),
        )(phase_label, grain_label, solute_init, grain_orient, orient_mobility, partition.T)

    placed = (P("grow", "trans", None), P("grow", "trans", None), P(), P(), P(None, "grow", "trans", None), P())
    return jax.shard_map(
        shards,
        mesh=mesh,
        in_specs=placed,
        out_specs=(P(None, "grow", "trans", None), P(None, "grow", "trans", None)),
        check_vma=False,
    )
```

time: 44.8 us -> 29.8 us (0.67)
  the two profiles are of different devices: /device:TPU:1 before, /device:TPU:473 now
where the time goes in v2:
time: 29.8 us; the launch traced here: 29.7 us
  Pallas kernels  27.7 us (93%)
  local copies, waits for them, and re-layouts  1.42 us (5%)
  between operations  0.64 us (2%)
    pallas_call x1, Pallas kernels, shards(): pl.pallas_call(functools.partial(kernel, n_grow, n_trans), out_shape=(plt...  27.7 us
    unnamed x2, local copies, waits for them, and re-layouts  1.42 us

profile of v2, /device:TPU:473, one launch (start us, length us, event | category | flops | bytes accessed | tf_op | source)
XLA Modules:
  0.0 29.7 jit_solution(4351263240689284775)
XLA Ops:
  0.6 27.7 %shard_map.77 = (f32[4,24,8,128]{3,2,1,0:T(8,128)S(1)}, f32[2,24,8,128]{3,2,1,0:T(8,128)S(1)}) custom-call(s32[24,8,128]{2,1,0:T(8,128)} %ph.1, s32[24,8,128]{2,1,0:T(8,128)} %gr.1, f32[2,24,8,128]{3,2,1,0:T(8,128)} %so.1, s32[32]{0:T(128)} %go_h.1, f32[8]{0:T(128)} %om_h.1, f32[2,4]{1,0:T(2,128)} %bitcast.1), custom_call_target="tpu_custom_call" | custom-call | tf_op jit(solution)/shard_map/pallas_call | solution.py:399
  28.3 0.7 %copy.10 = f32[4,24,8,128]{3,2,1,0:T(8,128)} copy(f32[4,24,8,128]{3,2,1,0:T(8,128)S(1)} %get-tuple-element.2) | data formatting | bytes 786432
  29.1 0.7 %copy.11 = f32[2,24,8,128]{3,2,1,0:T(8,128)} copy(f32[2,24,8,128]{3,2,1,0:T(8,128)S(1)} %get-tuple-element.3) | data formatting | bytes 393216

commit v3 on v2

--- a/solution.py
+++ b/solution.py
@@ -22,6 +22,7 @@
 LIQUID_MOBILITY = 1.0
 ROWS, OWN, NEXT = 24, 8, 16
 UNROLL_WIDE, UNROLL_SLIM = 3, 5
+TURN = 8
 SPLIT = 9
 
 
@@ -38,6 +39,8 @@
     far_left = jnp.logical_not(far_right)
     end = jnp.logical_or(place == 0, far_right)
     early = jnp.logical_and(end, t < half)
+    sooner = jnp.logical_and(early, lax.rem(g, TURN) == 0)
+    later = jnp.logical_and(early, lax.rem(g, TURN) != 0)
     own = planes - SHIFT + STEPS
     skip = planes - own
     more = SHIFT + STEPS
@@ -108,16 +111,15 @@
             pieces.append(group(pairs, dg, tt))
         return pieces
 
-    sp, dp = pl.ds(0, more), pl.ds(own, more)
-    main = group(
-        (
+    main = [None]
+    for src, size in ((0, SPLIT), (SPLIT, more - SPLIT)):
+        sp, dp = pl.ds(src, size), pl.ds(own + src, size)
+        pairs = (
             (ph.at[sp], PC.at[dp]),
             (so.at[:, sp], S0.at[pl.ds(4, 2), dp, pl.ds(OWN, rows)]),
             (gr.at[sp], GC.at[dp]),
-        ),
-        -1,
-        t,
-    )
+        )
+        main.append(group(pairs, -1, t))
     to_left = halo(PN, GN, SN, pl.ds(0, STEPS), pl.ds(0, STEPS - 1), left)
     to_right = halo(PL, GL, SL, pl.ds(rows - STEPS, STEPS), pl.ds(rows - STEPS + 1, STEPS - 1), right)
 
@@ -142,6 +144,12 @@
         def _():
             start_halo(to_right)
 
+    def start_main():
+        @pl.when(inner)
+        def _():
+            for copy in main[1] + main[2]:
+                copy.start()
+
     def start_near():
         @pl.when(far_left)
         def _():
@@ -151,10 +159,7 @@
         def _():
             start_halo(to_left)
 
-        @pl.when(inner)
-        def _():
-            for copy in main:
-                copy.start()
+        start_main()
 
     def meet():
         @pl.when(first)
@@ -216,9 +221,10 @@
     def roll(v, shift):
         return pltpu.roll(v, shift % v.shape[1], 1)
 
-    def advance(load, w, up, down, height, mob):
-        total = jnp.float32(n_grow * planes)
-        undercool = 2.0 * (0.5 - (height.astype(jnp.float32) + 0.5) / total)
+    def cooling(height):
+        return 2.0 * (0.5 - (height.astype(jnp.float32) + 0.5) / jnp.float32(n_grow * planes))
+
+    def advance(load, w, up, down, undercool, mob):
         centre = [load(k, w, 0) for k in range(6)]
         above = [load(k, up, 0) for k in range(6)]
         below = [load(k, down, 0) for k in range(6)]
@@ -262,7 +268,7 @@
             return S0[k, i, at]
 
         def body(w, _):
-            new = advance(load, w, jnp.minimum(w + 1, top), w - 1, origin + w, MO[w, pl.ds(row, size)])
+            new = advance(load, w, jnp.minimum(w + 1, top), w - 1, cooling(origin + w), MO[w, pl.ds(row, size)])
             for k in range(6):
                 T1[k, w, pl.ds(row, size)] = new[k]
             return 0
@@ -274,7 +280,7 @@
             return T1[k, i, pl.ds(row + by, size)]
 
         def body(w, _):
-            new = advance(load, w, jnp.minimum(w + 1, top), w - 1, origin + w, MO[w, pl.ds(row, size)])
+            new = advance(load, w, jnp.minimum(w + 1, top), w - 1, cooling(origin + w), MO[w, pl.ds(row, size)])
             for k in range(6):
                 T2[k, w, pl.ds(row, size)] = new[k]
             return 0
@@ -288,7 +294,7 @@
             return T2[k, i, pl.ds(OWN + by, rows)]
 
         def body(w, _):
-            new = advance(load, w, w + 1, jnp.maximum(w - 1, bottom), g * planes + w - STEPS, MO[w, pl.ds(OWN, rows)])
+            new = advance(load, w, w + 1, jnp.maximum(w - 1, bottom), cooling(g * planes + w - STEPS), MO[w, pl.ds(OWN, rows)])
             for k in range(4):
                 pout[k, w - STEPS] = new[k]
             for k in range(2):
@@ -340,48 +346,106 @@
     for copy in local[:3]:
         copy.wait()
     expand(0, own, OWN, PC, GC, None)
+
+    @pl.when(sooner)
+    def _():
+        meet()
+        start_far()
+
     take([0], always, True)
     take([0], middle, False)
     one(1, own - 1, OWN - 2, wide, UNROLL_WIDE)
     two(2, own - 2, OWN - 2, wide, UNROLL_WIDE)
 
-    @pl.when(early)
+    @pl.when(later)
     def _():
         meet()
         start_far()
 
-    @pl.when(outer)
-    def _():
-        arrive(main)
-
-    expand(own, length, OWN, PC, GC, None)
-    take([1, 2], always, True)
-    take([1, 2], middle, False)
-    one(own - 1, length - 1, OWN - 2, wide, UNROLL_WIDE)
-    two(own - 2, length - 2, OWN - 2, wide, UNROLL_WIDE)
-
-    near = jnp.where(far_right, NEXT + 2 - rows, OWN - 2)
     bounds = (1, own, own + SPLIT, length)
+
+    def lows(n):
+        return [max(bounds[n] - s, s) for s in (1, 2, 3)]
+
+    def shut(n):
+        if bounds[n + 1] - 2 > own:
+            flood(lows(n)[1], bounds[n + 1] - 2)
+
+    def finish(n):
+        shut(n)
+        three(lows(n)[2], bounds[n + 1] - 3, UNROLL_SLIM)
+
+    finish(0)
+
+    for n in (1, 2):
+
+        @pl.when(outer)
+        def _():
+            arrive(main[n])
+
+        expand(bounds[n], bounds[n + 1], OWN, PC, GC, None)
+        take([n], always, True)
+        take([n], middle, False)
+        one(lows(n)[0], bounds[n + 1] - 1, OWN - 2, wide, UNROLL_WIDE)
+        two(lows(n)[1], bounds[n + 1] - 2, OWN - 2, wide, UNROLL_WIDE)
+        finish(n)
+
+    quad = rows // 2
+    upper = lax.broadcasted_iota(jnp.int32, (rows, cols), 0) < quad
+
+    def pairs(low, high, source, row, above, below, height, store):
+        def load(k, planes_of, by):
+            ref = MO if k is None else source.at[k]
+            return jnp.where(upper, ref[planes_of[0], pl.ds(row + by, rows)], ref[planes_of[1], pl.ds(row + by - quad, rows)])
+
+        def body(n, _):
+            w = low + 2 * n
+            undercool = jnp.where(upper, cooling(height + w), cooling(height + w + 1))
+            here = (w, w + 1)
+            new = advance(load, here, (above(w), above(w + 1)), (below(w), below(w + 1)), undercool, load(None, here, 0))
+            for k in range(6):
+                store(k, w, new[k][:quad])
+                store(k, w + 1, new[k][quad:])
+            return 0
+
+        count = (high - low + 1) // 2
+        lax.fori_loop(0, count, body, 0, unroll=count)
+
+    def keep(ref, row):
+        def store(k, w, value):
+            ref[k, w, pl.ds(row, quad)] = value
+
+        return store
+
+    def emit(k, w, value):
+        at = pl.ds(jnp.where(far_right, quad, 0), quad)
+        if k < 4:
+            pout[k, w - STEPS, at] = value
+        else:
+            sout[k - 4, w - STEPS, at] = value
+
+    rows_of = [jnp.where(far_right, NEXT + 2 - quad - s, OWN - 2 + s) for s in range(3)]
+
+    def capped(w):
+        return jnp.minimum(w + 1, top)
+
     for n in range(3):
-        high = bounds[n + 1]
-        lows = [max(bounds[n] - s, s) for s in (1, 2, 3)]
         take([n], end, False)
 
         @pl.when(end)
         def _():
-            one(lows[0], high - 1, near, rows, UNROLL_SLIM)
-            two(lows[1], high - 2, near, rows, UNROLL_SLIM)
-
-        if high - 2 > own:
-            flood(lows[1], high - 2)
-        three(lows[2], high - 3, UNROLL_SLIM)
+            low, high = lows(n), bounds[n + 1]
+            pairs(low[0], high - 1, S0, rows_of[0], capped, lambda w: w - 1, origin, keep(T1, rows_of[0]))
+            pairs(low[1], high - 2, T1, rows_of[1], capped, lambda w: w - 1, origin, keep(T2, rows_of[1]))
+            shut(n)
+            pairs(low[2], high - 3, T2, rows_of[2], lambda w: w + 1, lambda w: jnp.maximum(w - 1, bottom), g * planes - STEPS, emit)
 
     for copy in to_left[0] + to_right[0]:
         copy.wait_send()
 
     @pl.when(inner)
     def _():
-        for copy in main + to_left[1] + to_left[2] + to_right[1] + to_right[2]:
+        for copy in main[1] + main[2] + to_left[1] + to_left[2] + to_right[1] + to_right[2]:
             copy.wait_send()
 
 
@@ -422,8 +486,8 @@
                 pltpu.SMEM(orient_mobility.shape, f32),
                 pltpu.SMEM(partition.shape[::-1], f32),
                 pltpu.SemaphoreType.DMA((6,)),
-                pltpu.SemaphoreType.DMA((21,)),
-                pltpu.SemaphoreType.DMA((21,)),
+                pltpu.SemaphoreType.DMA((24,)),
+                pltpu.SemaphoreType.DMA((24,)),
                 pltpu.SemaphoreType.REGULAR,
             ],
             compiler_params=pltpu.CompilerParams(collective_id=0, has_side_effects=True),

time: 29.8 us -> 26.8 us (0.90)
  the two profiles are of different devices: /device:TPU:473 before, /device:TPU:97 now
where the time goes in v3:
time: 26.8 us; the launch traced here: 26.6 us
  Pallas kernels  24.6 us (92%)
  local copies, waits for them, and re-layouts  1.42 us (5%)
  between operations  0.64 us (2%)
    pallas_call x1, Pallas kernels, shards(): pl.pallas_call(functools.partial(kernel, n_grow, n_trans), out_shape=(plt...  24.6 us
    unnamed x2, local copies, waits for them, and re-layouts  1.42 us

profile of v3, /device:TPU:97, one launch (start us, length us, event | category | flops | bytes accessed | tf_op | source)
XLA Modules:
  0.0 26.6 jit_solution(11543771545994460060)
XLA Ops:
  0.6 24.6 %shard_map.77 = (f32[4,24,8,128]{3,2,1,0:T(8,128)S(1)}, f32[2,24,8,128]{3,2,1,0:T(8,128)S(1)}) custom-call(s32[24,8,128]{2,1,0:T(8,128)} %ph.1, s32[24,8,128]{2,1,0:T(8,128)} %gr.1, f32[2,24,8,128]{3,2,1,0:T(8,128)} %so.1, s32[32]{0:T(128)} %go_h.1, f32[8]{0:T(128)} %om_h.1, f32[2,4]{1,0:T(2,128)} %bitcast.1), custom_call_target="tpu_custom_call" | custom-call | tf_op jit(solution)/shard_map/pallas_call | solution.py:463
  25.2 0.7 %copy.10 = f32[4,24,8,128]{3,2,1,0:T(8,128)} copy(f32[4,24,8,128]{3,2,1,0:T(8,128)S(1)} %get-tuple-element.2) | data formatting | bytes 786432
  26.0 0.7 %copy.11 = f32[2,24,8,128]{3,2,1,0:T(8,128)} copy(f32[2,24,8,128]{3,2,1,0:T(8,128)S(1)} %get-tuple-element.3) | data formatting | bytes 393216

commit v4 on v3

--- a/solution.py
+++ b/solution.py
@@ -22,6 +22,7 @@
 LIQUID_MOBILITY = 1.0
 ROWS, OWN, NEXT = 24, 8, 16
 UNROLL_WIDE, UNROLL_SLIM = 3, 5
+PARTS = 6
 TURN = 8
 SPLIT = 9
 
@@ -449,6 +450,15 @@
             copy.wait_send()
 
 
+def put_out(phases, solutes, pout, sout, done):
+    pieces = [(phases.at[k], pout.at[k]) for k in range(4)] + [(solutes.at[k], sout.at[k]) for k in range(2)]
+    copies = [pltpu.make_async_copy(src, dst, done.at[n]) for n, (src, dst) in enumerate(pieces)]
+    for copy in copies:
+        copy.start()
+    for copy in copies:
+        copy.wait()
+
+
 def solution(mesh):
     n_grow, n_trans = mesh.shape["grow"], mesh.shape["trans"]
 
@@ -460,7 +470,7 @@
         hbm = pl.BlockSpec(memory_space=pl.ANY)
         vmem = pl.BlockSpec(memory_space=pltpu.VMEM)
         f32, i32 = jnp.float32, jnp.int32
-        return pl.pallas_call(
+        results = pl.pallas_call(
             functools.partial(kernel, n_grow, n_trans),
             out_shape=(
                 pltpu.VMEM((4, planes, rows, cols), f32),
@@ -492,6 +502,13 @@
             ],
             compiler_params=pltpu.CompilerParams(collective_id=0, has_side_effects=True),
         )(phase_label, grain_label, solute_init, grain_orient, orient_mobility, partition.T)
+        return pl.pallas_call(
+            put_out,
+            out_shape=tuple(jax.ShapeDtypeStruct(r.shape, r.dtype) for r in results),
+            in_specs=[vmem, vmem],
+            out_specs=(hbm, hbm),
+            scratch_shapes=[pltpu.SemaphoreType.DMA((PARTS,))],
+        )(*[pltpu.with_memory_space_constraint(r, pltpu.VMEM) for r in results])
 
     placed = (P("grow", "trans", None), P("grow", "trans", None), P(), P(), P(None, "grow", "trans", None), P())
     return jax.shard_map(

time: 26.8 us -> 26.2 us (0.978)
  local copies, waits for them, and re-layouts: 1.42 us -> 0 us
  Pallas kernels: 24.6 us -> 25.4 us
    unnamed x2 -> x0, local copies, waits for them, and re-layouts: 1.42 us -> none
    pallas_call x0 -> x1, Pallas kernels: none -> 0.86 us  [shards(): pl.pallas_call(put_out, out_shape=tuple((jax.ShapeDtypeStruct(r.shape, r....]
where the time goes in v4:
time: 26.2 us; the launch traced here: 26.1 us
  Pallas kernels  25.4 us (97%)
  between operations  0.64 us (2%)
    pallas_call x1, Pallas kernels, shards(): pl.pallas_call(functools.partial(kernel, n_grow, n_trans), out_shape=(plt...  24.6 us
    pallas_call x1, Pallas kernels, shards(): pl.pallas_call(put_out, out_shape=tuple((jax.ShapeDtypeStruct(r.shape, r....  0.86 us

profile of v4, /device:TPU:97, one launch (start us, length us, event | category | flops | bytes accessed | tf_op | source)
XLA Modules:
  0.0 26.1 jit_solution(8763497126977762848)
XLA Ops:
  0.6 24.6 %shard_map.77 = (f32[4,24,8,128]{3,2,1,0:T(8,128)S(1)}, f32[2,24,8,128]{3,2,1,0:T(8,128)S(1)}) custom-call(s32[24,8,128]{2,1,0:T(8,128)} %ph.1, s32[24,8,128]{2,1,0:T(8,128)} %gr.1, f32[2,24,8,128]{3,2,1,0:T(8,128)} %so.1, s32[32]{0:T(128)} %go_h.1, f32[8]{0:T(128)} %om_h.1, f32[2,4]{1,0:T(2,128)} %bitcast.1), custom_call_target="tpu_custom_call" | custom-call | tf_op jit(solution)/shard_map/pallas_call | solution.py:473
  25.2 0.9 %shard_map.78 = (f32[4,24,8,128]{3,2,1,0:T(8,128)}, f32[2,24,8,128]{3,2,1,0:T(8,128)}) custom-call(f32[4,24,8,128]{3,2,1,0:T(8,128)S(1)} %get-tuple-element.4.phases, f32[2,24,8,128]{3,2,1,0:T(8,128)S(1)} %get-tuple-element.5.solutes), custom_call_target="tpu_custom_call" | custom-call | tf_op jit(solution)/shard_map/pallas_call | solution.py:505

commit v5 on v4

--- a/solution.py
+++ b/solution.py
@@ -152,6 +152,8 @@
                 copy.start()
 
     def start_near():
+        start_main()
+
         @pl.when(far_left)
         def _():
             start_halo(to_right)
@@ -160,7 +162,6 @@
         def _():
             start_halo(to_left)
 
-        start_main()
 
     def meet():
         @pl.when(first)

time: 26.2 us -> 26.2 us (level)
  no operation moved by 1% of the time
where the time goes in v5:
time: 26.2 us; the launch traced here: 26.1 us
  Pallas kernels  25.4 us (97%)
  between operations  0.64 us (2%)
    pallas_call x1, Pallas kernels, shards(): pl.pallas_call(functools.partial(kernel, n_grow, n_trans), out_shape=(plt...  24.6 us
    pallas_call x1, Pallas kernels, shards(): pl.pallas_call(put_out, out_shape=tuple((jax.ShapeDtypeStruct(r.shape, r....  0.86 us

profile of v5, /device:TPU:97, one launch (start us, length us, event | category | flops | bytes accessed | tf_op | source)
XLA Modules:
  0.0 26.1 jit_solution(15156196026441413894)
XLA Ops:
  0.6 24.6 %shard_map.77 = (f32[4,24,8,128]{3,2,1,0:T(8,128)S(1)}, f32[2,24,8,128]{3,2,1,0:T(8,128)S(1)}) custom-call(s32[24,8,128]{2,1,0:T(8,128)} %ph.1, s32[24,8,128]{2,1,0:T(8,128)} %gr.1, f32[2,24,8,128]{3,2,1,0:T(8,128)} %so.1, s32[32]{0:T(128)} %go_h.1, f32[8]{0:T(128)} %om_h.1, f32[2,4]{1,0:T(2,128)} %bitcast.1), custom_call_target="tpu_custom_call" | custom-call | tf_op jit(solution)/shard_map/pallas_call | solution.py:474
  25.2 0.9 %shard_map.78 = (f32[4,24,8,128]{3,2,1,0:T(8,128)}, f32[2,24,8,128]{3,2,1,0:T(8,128)}) custom-call(f32[4,24,8,128]{3,2,1,0:T(8,128)S(1)} %get-tuple-element.4.phases, f32[2,24,8,128]{3,2,1,0:T(8,128)S(1)} %get-tuple-element.5.solutes), custom_call_target="tpu_custom_call" | custom-call | tf_op jit(solution)/shard_map/pallas_call | solution.py:506
